TPU v7x, 128 devices: a whole 4x4x4 slice. The times are simulated.
128 devices in a mesh: blk: 4 (over x), tok: 32 (over y, z, core).
Axes of the slice: x: 4, y: 4, z: 4, core: 2. Of those that a mesh axis runs over, the one named last changes fastest.
Arguments:
- tokens: bfloat16 [32, 1024, 1664], P('tok', 'blk'), may hold values from -6 to 6
- segment_ids: int32 [32, 1024], P('tok'), may hold values from 0 to 31, as said below
- merge_index: int32 [32, 256, 4], P('tok'), may hold values from 0 to 1023, as said below
- segment_owner: int32 [32, 32], P('tok'), may hold values from 0 to 31, each once within a row
- ln1_gain: float32 [1664], replicated, may hold values from 0.1 to 1.9
- ln1_bias: float32 [1664], replicated, may hold values from -4 to 4
- w_qkv: bfloat16 [3, 1664, 1664], P(None, 'tok', 'blk'), may hold values from -0.15625 to 0.15625
- qkv_bias: float32 [3, 1664], P(None, 'blk'), may hold values from -6 to 6
- w_out: bfloat16 [1664, 1664], P('blk', 'tok'), may hold values from -0.15625 to 0.15625
- out_bias: float32 [1664], replicated, may hold values from -6 to 6
- ln2_gain: float32 [1664], replicated, may hold values from 0.1 to 1.9
- ln2_bias: float32 [1664], replicated, may hold values from -4 to 4
- w_fc1: bfloat16 [1664, 8192], P(None, 'blk'), may hold values from -0.15625 to 0.15625
- fc1_bias: float32 [8192], P('blk'), may hold values from -6 to 6
- w_fc2: bfloat16 [8192, 1664], P('blk'), may hold values from -0.0625 to 0.0625
- fc2_bias: float32 [1664], replicated, may hold values from -6 to 6
- ln3_gain: float32 [1664], replicated, may hold values from 0.1 to 1.9
- ln3_bias: float32 [1664], replicated, may hold values from -4 to 4
- w_proj: bfloat16 [6656, 1664], P('tok', 'blk'), may hold values from -0.078125 to 0.078125
- proj_bias: float32 [1664], P('blk'), may hold values from -6 to 6
Outputs:
- returned: bfloat16 [32, 32, 16, 1664], P('tok', None, None, 'blk')
Inputs may be any that keep to these rules, and one draw needn't show every extreme that they name: `segment_ids`: within a block each segment holds 4 to 64 tokens, one exactly 64; the four tokens of one row of merge_index share a segment. `merge_index`: the rows of one block name each token of the block exactly once. `segment_owner`: each block's row is a permutation of the owners.
All inputs are finite; a program needn't handle non-finite values.
Results may differ from a plain program's by a relative error of at most 0.015.
Values may be sent and summed in bfloat16 or wider, within the bound.
A program may use at most 128 MiB of HBM per device.

v0:
```python
import math
import jax
import jax.numpy as jnp
from jax import lax
from jax.sharding import PartitionSpec as P

HD = 104
EPS = 1e-06


def layer_norm(input_tensors, scales, offset):
    input_tensors = input_tensors.astype(jnp.float32)
    center = input_tensors - jnp.mean(input_tensors, axis=-1, keepdims=True)
    spread = jnp.mean(center * center, axis=-1, keepdims=True)
    return center * lax.rsqrt(spread + EPS) * scales + offset


def body(
    tokens,
    segment_ids,
    merge_index,
    segment_owner,
    ln1_gain,
    ln1_bias,
    w_qkv,
    qkv_bias,
    w_out,
    out_bias,
    ln2_gain,
    ln2_bias,
    w_fc1,
    fc1_bias,
    w_fc2,
    fc2_bias,
    ln3_gain,
    ln3_bias,
    w_proj,
    proj_bias,
):
    tok_block = tokens[0]
    row_count = tok_block.shape[0]
    model_width = tok_block.shape[1]
    head_cols = w_qkv.shape[2]
    heads_here = head_cols // HD
    normed_one = layer_norm(tok_block, ln1_gain, ln1_bias).astype(jnp.bfloat16)
    normed_all = lax.all_gather(normed_one, "blk", axis=0, tiled=True)
    all_rows = normed_all.shape[0]
    columns = normed_all
    projected_qkv = jnp.einsum(
        "td,cde->cte",
        columns,
        lax.all_gather(w_qkv, "tok", axis=1, tiled=True),
        preferred_element_type=jnp.float32,
    )
    projected_qkv = (projected_qkv + qkv_bias[:, None, :]).astype(jnp.bfloat16)
    projected_qkv = projected_qkv.reshape(3, all_rows, heads_here, HD)
    key_rows = projected_qkv[1]
    values = projected_qkv[2]
    segment_row = segment_ids[0]
    q_block = min(512, all_rows)
    block_count = all_rows // q_block
    query_rows = projected_qkv[0].reshape(block_count, q_block, heads_here, HD)
    query_segs = segment_row.reshape(block_count, q_block)
    score_scale = 1.0 / math.sqrt(HD)

    def attend(input_tensors):
        query_part, query_seg = input_tensors
        scores = (
            jnp.einsum("qhe,khe->hqk", query_part, key_rows, preferred_element_type=jnp.float32)
            * score_scale
        )
        allowed = query_seg[:, None] == segment_row[None, :]
        weights = jnp.where(allowed[None], jnp.exp(scores), 0.0)
        attn_probs = (weights / jnp.sum(weights, axis=-1, keepdims=True)).astype(jnp.bfloat16)
        mixed = jnp.einsum("hqk,khe->qhe", attn_probs, values, preferred_element_type=jnp.float32)
        return mixed.astype(jnp.bfloat16)

    attended = lax.map(attend, (query_rows, query_segs)).reshape(all_rows, head_cols)
    out_full = lax.all_gather(w_out, "tok", axis=1, tiled=True)
    attn_rows = lax.psum_scatter(
        jnp.dot(attended, out_full, preferred_element_type=jnp.float32).astype(jnp.bfloat16),
        "blk",
        scatter_dimension=0,
        tiled=True,
    ).astype(jnp.float32)
    after_attn = tok_block.astype(jnp.float32) + attn_rows + out_bias
    normed_two = layer_norm(after_attn, ln2_gain, ln2_bias).astype(jnp.bfloat16)
    pre_act = (
        jnp.dot(
            lax.all_gather(normed_two, "blk", axis=0, tiled=True),
            w_fc1,
            preferred_element_type=jnp.float32,
        )
        + fc1_bias
    )
    hidden_act = jax.nn.gelu(pre_act, approximate=False).astype(jnp.bfloat16)
    partial_sum = jnp.dot(hidden_act, w_fc2, preferred_element_type=jnp.float32)
    own_start = lax.axis_index("blk") * row_count
    own_rows = lax.dynamic_slice_in_dim(partial_sum, own_start, row_count, 0) + after_attn
    partial_sum = lax.dynamic_update_slice_in_dim(partial_sum, own_rows, own_start, 0)
    summed = lax.psum(partial_sum.astype(jnp.bfloat16), "blk").astype(jnp.float32)
    layer_all = (summed + fc2_bias).astype(jnp.bfloat16)
    final_all = layer_norm(layer_all, ln3_gain, ln3_bias).astype(jnp.bfloat16)
    merge_rows = merge_index[0]
    merged_count = merge_rows.shape[0]
    merged = jnp.take(final_all, merge_rows.reshape(-1), axis=0).reshape(
        merged_count, 4 * model_width
    )
    columns = merged
    projected = jnp.dot(
        columns,
        lax.all_gather(w_proj, "tok", axis=0, tiled=True),
        preferred_element_type=jnp.float32,
    )
    projected = (projected + proj_bias).astype(jnp.bfloat16)
    tok_count = lax.axis_size("tok")
    slot_cap = 2 * merged_count // tok_count
    owners_here = segment_owner[0]
    seg_rows = jnp.take(segment_row, merge_rows[:, 0])
    seg_match = (
        seg_rows[:, None] == jnp.arange(owners_here.shape[0], dtype=jnp.int32)[None, :]
    ).astype(jnp.int32)
    owner_rows = jnp.sum(seg_match * owners_here[None, :], axis=1)
    segment_matches = (
        owner_rows[:, None] == jnp.arange(tok_count, dtype=jnp.int32)[None, :]
    ).astype(jnp.int32)
    before = jnp.cumsum(segment_matches, axis=0) - segment_matches
    order_in = jnp.sum(before * segment_matches, axis=1)
    target = owner_rows * slot_cap + order_in
    placed = (jnp.arange(tok_count * slot_cap, dtype=jnp.int32)[:, None] == target[None, :]).astype(
        jnp.bfloat16
    )
    outgoing = jnp.dot(placed, projected, preferred_element_type=jnp.float32).astype(jnp.bfloat16)
    outgoing = outgoing.reshape(tok_count, slot_cap, projected.shape[1])
    arrived = lax.all_to_all(outgoing, "tok", split_axis=0, concat_axis=0, tiled=True)
    return arrived[None]


def solution(mesh):
    placed = (
        P("tok", "blk", None),
        P("tok", None),
        P("tok", None, None),
        P("tok", None),
        P(),
        P(),
        P(None, "tok", "blk"),
        P(None, "blk"),
        P("blk", "tok"),
        P(),
        P(),
        P(),
        P(None, "blk"),
        P("blk"),
        P("blk", None),
        P(),
        P(),
        P(),
        P("tok", "blk"),
        P("blk"),
    )
    return jax.shard_map(
        body, mesh=mesh, in_specs=placed, out_specs=P("tok", None, None, "blk"), check_vma=False
    )
```

profile of v0, /device:TPU:1, one launch (start us, length us, event | category | flops | bytes accessed | tf_op | source)
XLA Modules:
  0.0 480.8 jit_solution(5821261523930769322)
XLA Ops:
  6.5 0.7 all-gather.15.cloned.1.call-update
  7.3 0.0 all-gather.7.cloned.1.call-start
  7.3 1.3 convert_reduce_fusion.1
  8.7 1.5 fusion.43
  10.2 2.5 fusion.46
  12.8 0.0 all-gather.9.cloned.1.call-start
  12.8 1.7 copy.32
  14.5 0.0 reduce-scatter.2.cloned.1.call-start
  14.6 0.5 broadcast.197
  15.1 1.3 reduce.6
  16.4 40.5 %all-gather.15.cloned.1.call-done = bf16[32,52,416]{2,1,0:T(8,128)(2,1)} async-done(((bf16[1,52,416]{2,1,0:T(8,128)(2,1)}), bf16[32,52,416]{2,1,0:T(8,128)(2,1)}) %all-gather.15.cloned.1.call-update) | async-done | bytes 1384464 | tf_op jit(solution)/shard_map/all_gather | solution.py:79
  56.9 2.7 reshape.179
  59.7 39.4 %all-gather.7.cloned.1.call-done = bf16[1024,1664]{1,0:T(8,128)(2,1)} async-done(((bf16[256,1664]{1,0:T(8,128)(2,1)}), bf16[1024,1664]{1,0:T(8,128)(2,1)}) %all-gather.7.cloned.1.call-update) | async-done | bytes 3407888 | tf_op jit(solution)/shard_map/all_gather | solution.py:46
  99.1 53.1 %all-gather.9.cloned.1.call-done = bf16[3,1664,416]{2,0,1:T(4,128)(2,1)} async-done(((bf16[3,52,416]{2,0,1:T(4,128)(2,1)}), bf16[3,1664,416]{2,0,1:T(4,128)(2,1)}) %all-gather.9.cloned.1.call-update) | async-done | bytes 4153360 | tf_op jit(solution)/shard_map/all_gather | solution.py:52
  152.2 9.2 %fusion.34 = bf16[3,1024,416]{1,2,0:T(8,128)(2,1)S(1)} fusion(f32[3,416]{1,0:T(4,128)S(1)} %copy-done.15, bf16[3,1664,416]{2,0,1:T(4,128)(2,1)} %all-gather.9.cloned.1.call-done, bf16[1024,1664]{1,0:T(8,128)(2,1)} %all-gather.7.cloned.1.call-done), kind=kOutput, calls=%fused_computation.53 | convolution fusion | flops 4255580160 | bytes 10122112 | tf_op jit(solution)/shard_map/td,cde->cte/dot_general | solution.py:49
  161.4 1.4 fusion.96
  162.8 0.6 reshape_squeeze.10
  163.4 1.0 copy.34
  164.4 15.8 %while.10 = (s32[]{:T(128)}, bf16[2,512,4,104]{1,3,2,0:T(8,128)(2,1)}, s32[2,512]{1,0:T(2,128)S(1)}, s32[1,1024]{1,0:T(1,128)S(1)}, bf16[2,512,4,104]{1,3,2,0:T(...) while((s32[]{:T(128)}, bf16[2,512,4,104]{1,3,2,0:T(8,128)(2,1)}, ...), condition=%wide.region_8.9_spmd, body=%wide.region_6.8_spmd.sunk | while | flops 887830528 | bytes 31156912 | solution.py:78
  164.4 0.4 broadcast_compare_fusion.2
  164.8 4.0 fusion.112
  168.8 2.5 fusion.113
  171.3 0.9 copy-done.6
  172.3 0.4 broadcast_compare_fusion.2
  172.6 4.0 fusion.112
  176.6 2.5 fusion.113
  179.2 0.9 copy-done.6
  180.2 2.0 copy.35
  182.2 0.2 copy.40
  182.4 3.9 convolution_convert_fusion
  186.4 0.0 all-gather.11.cloned.1.call-start
  186.4 38.9 %reduce-scatter.2.cloned.1.call-done = bf16[256,1664]{1,0:T(8,128)(2,1)} async-done(((bf16[1024,1664]{1,0:T(8,128)(2,1)}), bf16[256,1664]{1,0:T(8,128)(2,1)}) %reduce-scatter.2.cloned.1.call-update) | async-done | bytes 851984 | tf_op jit(solution)/shard_map/reduce_scatter | solution.py:80
  225.3 1.5 fusion.57
  226.9 1.7 multiply_reduce_fusion
  228.5 2.6 add_convert_fusion.2
  231.2 0.0 all-reduce.2.cloned.1.call-start
  231.3 41.5 %all-gather.11.cloned.1.call-done = bf16[1024,1664]{1,0:T(8,128)(2,1)} async-done(((bf16[256,1664]{1,0:T(8,128)(2,1)}), bf16[1024,1664]{1,0:T(8,128)(2,1)}) %all-gather.11.cloned.1.call-update) | async-done | bytes 3407888 | tf_op jit(solution)/shard_map/all_gather | solution.py:90
  272.7 11.1 %fusion.97 = f32[1024,2048]{1,0:T(8,128)S(1)} fusion(bf16[1024,1664]{1,0:T(8,128)(2,1)} %all-gather.11.cloned.1.call-done, bf16[1664,2048]{1,0:T(8,128)(2,1)} %param.34), kind=kOutput, calls=%fused_computation.133 | convolution fusion | flops 6979321856 | bytes 18612224 | tf_op jit(solution)/shard_map/dot_general | solution.py:89
  283.9 28.8 %fusion.29 = f32[1024,1664]{1,0:T(8,128)S(1)} fusion(bf16[2048,1664]{1,0:T(8,128)(2,1)} %param.36, f32[1024,2048]{1,0:T(8,128)S(1)} %fusion.97, f32[2048]{0:T(1024)S(1)} %copy-done.16), kind=kOutput, calls=%fused_computation.48 | convolution fusion | flops 7117733888 | bytes 22028288 | tf_op jit(solution)/shard_map/dot_general | solution.py:97
  312.8 0.4 add_dynamic-update-slice_fusion
  313.2 2.2 convert_element_type.78
  315.4 0.0 all-gather.13.cloned.1.call-start
  315.5 0.7 all-gather.13.cloned.1.call-update
  316.2 0.1 copy.36
  316.4 0.1 reshape_squeeze.11
  316.5 1.4 gather_fusion
  317.9 0.1 select_reduce_fusion
  318.0 0.6 reduce-window.6
  318.6 0.2 slice_reduce_fusion
  318.8 0.2 copy.31
  319.0 0.9 broadcast_in_dim.40
  320.0 2.0 copy.39
  322.0 0.1 fusion.62
  322.1 73.7 %all-reduce.2.cloned.1.call-done = bf16[1024,1664]{1,0:T(8,128)(2,1)} async-done(((bf16[1024,1664]{1,0:T(8,128)(2,1)}), bf16[1024,1664]{1,0:T(8,128)(2,1)}) %all-reduce.2.cloned.1.call-update) | async-done | bytes 3407888 | tf_op jit(solution)/shard_map/psum | solution.py:101
  395.8 2.8 convert_reduce_fusion
  398.7 3.2 fusion.23
  401.9 1.8 fusion.26
  403.7 5.9 %gather_fusion.1 = bf16[1024,1664]{1,0:T(8,128)(2,1)} fusion(bf16[1024,1664]{1,0:T(8,128)(2,1)S(1)} %fusion.26, s32[1024]{0:T(1024)S(1)} %broadcast_clamp_fusion), kind=kCustom, calls=%fused_computation.1 | custom fusion | bytes 6819840 | tf_op jit(solution)/shard_map/jit(_take)/gather | solution.py:106
  409.6 5.4 %gather.15 = bf16[256,6656]{1,0:T(8,128)(2,1)S(1)} reshape(bf16[1024,1664]{1,0:T(8,128)(2,1)} %gather_fusion.1) | data formatting | bytes 6815744 | tf_op jit(solution)/shard_map/jit(_take)/gather | solution.py:106
  415.0 33.5 %all-gather.13.cloned.1.call-done = bf16[6656,416]{1,0:T(8,128)(2,1)} async-done(((bf16[208,416]{1,0:T(8,128)(2,1)}), bf16[6656,416]{1,0:T(8,128)(2,1)}) %all-gather.13.cloned.1.call-update) | async-done | bytes 5537808 | tf_op jit(solution)/shard_map/all_gather | solution.py:112
  448.5 7.0 %convolution_convert_fusion.1 = bf16[512,416]{0,1:T(8,128)(2,1)} fusion(bf16[6656,416]{1,0:T(8,128)(2,1)} %all-gather.13.cloned.1.call-done, pred[256,6656]{1,0:T(8,128)(4,1)} %bitcast.118, bf16[256,6656]{1,0:T(8,128)(2,1)S(1)} %gather.15, s32[256]{0:T(256)S(1)} %multiply_add_fusion, f32[416]{0:T(512)S(1)} %copy-done.17), kind=kOutput, calls=%fused_computation.69 | convolution fusion | flops 1528987648 | bytes 11078272 | tf_op jit(solution)/shard_map/dot_general | solution.py:133
  455.5 1.2 copy.37
  456.7 16.2 %all_to_all.5 = bf16[32,16,416]{2,1,0:T(8,128)(2,1)S(1)} all-to-all(bf16[32,16,416]{2,1,0:T(8,128)(2,1)S(1)} %bitcast.116), channel_id=1, replica_groups=mesh['blk'=4,'tok'=32] {'tok'}, dimensions={0} | all-to-all | bytes 851968 | tf_op jit(solution)/shard_map/all_to_all | solution.py:135
  472.9 0.8 copy.56
  (66 shorter events, 0.3 us)
Async XLA Ops:
  6.5 145.7 %copy-start.15 = (f32[3,416]{1,0:T(4,128)S(1)}, f32[3,416]{1,0:T(4,128)}, u32[]{:S(2)}) copy-start(f32[3,416]{1,0:T(4,128)} %param.29) | copy-start | bytes 14980
  6.5 50.4 %all-gather.15.cloned.1.call-start = ((), (), s32[]{:S(2)}) async-start(), calls=%async_computation.8 | async-start | bytes 1892352 | tf_op jit(solution)/shard_map/all_gather | solution.py:79
  7.3 91.8 %all-gather.7.cloned.1.call-start = ((), (), s32[]{:S(2)}) async-start(), calls=%async_computation.2 | async-start | bytes 4259840 | tf_op jit(solution)/shard_map/all_gather | solution.py:46
  12.8 139.4 %all-gather.9.cloned.1.call-start = ((), (), s32[]{:S(2)}) async-start(), calls=%async_computation.3 | async-start | bytes 7028736 | tf_op jit(solution)/shard_map/all_gather | solution.py:52
  14.5 210.8 %reduce-scatter.2.cloned.1.call-start = ((), (), s32[]{:S(2)}) async-start(), calls=%async_computation.4 | async-start | bytes 4259840 | tf_op jit(solution)/shard_map/reduce_scatter | solution.py:80
  161.4 3.0 copy-start
  164.4 4.3 copy-start.4
  164.4 4.3 copy-start.5
  171.3 0.9 copy-start.6
  172.2 4.3 copy-start.4
  172.2 4.3 copy-start.5
  179.1 0.9 copy-start.6
  182.4 42.9 %copy-start.1 = (bf16[1,256,1664]{2,1,0:T(8,128)(2,1)S(1)}, bf16[1,256,1664]{2,1,0:T(8,128)(2,1)}, u32[]{:S(2)}) copy-start(bf16[1,256,1664]{2,1,0:T(8,128)(2,1)} %param.22) | copy-start | bytes 2555908
  182.4 42.9 %copy-start.7 = (f32[1664]{0:T(1024)S(1)}, f32[1664]{0:T(1024)}, u32[]{:S(2)}) copy-start(f32[1664]{0:T(1024)} %param.31) | copy-start | bytes 19972
  186.4 42.2 %copy-start.10 = (f32[1664]{0:T(1024)S(1)}, f32[1664]{0:T(1024)}, u32[]{:S(2)}) copy-start(f32[1664]{0:T(1024)} %param.33) | copy-start | bytes 19972
  186.4 42.2 %copy-start.11 = (f32[1664]{0:T(1024)S(1)}, f32[1664]{0:T(1024)}, u32[]{:S(2)}) copy-start(f32[1664]{0:T(1024)} %param.32) | copy-start | bytes 19972
  186.4 86.3 %all-gather.11.cloned.1.call-start = ((), (), s32[]{:S(2)}) async-start(), calls=%async_computation.5 | async-start | bytes 4259840 | tf_op jit(solution)/shard_map/all_gather | solution.py:90
  231.2 164.6 %all-reduce.2.cloned.1.call-start = ((), (), s32[]{:S(2)}) async-start(), calls=%async_computation.6 | async-start | bytes 6815744 | tf_op jit(solution)/shard_map/psum | solution.py:101
  231.2 52.6 %copy-start.16 = (f32[2048]{0:T(1024)S(1)}, f32[2048]{0:T(1024)}, u32[]{:S(2)}) copy-start(f32[2048]{0:T(1024)} %param.35) | copy-start | bytes 24580
  283.9 28.9 %copy-start.3 = (bf16[256,1664]{1,0:T(8,128)(2,1)S(1)}, bf16[256,1664]{1,0:T(8,128)(2,1)}, u32[]{:S(2)}) copy-start(bf16[256,1664]{1,0:T(8,128)(2,1)} %reduce-scatter.2.cloned.1.call-done) | copy-start | bytes 2555908
  313.2 3.0 copy-start.9
  313.2 4.7 copy-start.14
  315.4 80.4 %copy-start.8 = (f32[1664]{0:T(1024)S(1)}, f32[1664]{0:T(1024)}, u32[]{:S(2)}) copy-start(f32[1664]{0:T(1024)} %param.37) | copy-start | bytes 19972
  315.4 133.1 %all-gather.13.cloned.1.call-start = ((), (), s32[]{:S(2)}) async-start(), calls=%async_computation.7 | async-start | bytes 7028736 | tf_op jit(solution)/shard_map/all_gather | solution.py:112
  316.2 85.7 %copy-start.12 = (f32[1664]{0:T(1024)S(1)}, f32[1664]{0:T(1024)}, u32[]{:S(2)}) copy-start(f32[1664]{0:T(1024)} %param.39) | copy-start | bytes 19972
  316.2 85.6 %copy-start.13 = (f32[1664]{0:T(1024)S(1)}, f32[1664]{0:T(1024)}, u32[]{:S(2)}) copy-start(f32[1664]{0:T(1024)} %param.38) | copy-start | bytes 19972
  395.8 6.1 %copy-start.2 = (bf16[1024,1664]{1,0:T(8,128)(2,1)S(1)}, bf16[1024,1664]{1,0:T(8,128)(2,1)}, u32[]{:S(2)}) copy-start(bf16[1024,1664]{1,0:T(8,128)(2,1)} %all-reduce.2.cloned.1.call-done) | copy-start | bytes 10223620
  409.6 39.0 %copy-start.17 = (f32[416]{0:T(512)S(1)}, f32[416]{0:T(512)}, u32[]{:S(2)}) copy-start(f32[416]{0:T(512)} %param.41) | copy-start | bytes 4996
Sparse Core Ops, SparseCore 0:
  9.6 47.2 all-gather.14
  58.6 40.4 all-gather.6
  101.3 50.8 all-gather.8
  186.5 38.7 reduce-scatter.1
  231.3 41.3 all-gather.10
  315.5 80.1 all-reduce.1
  398.0 50.4 all-gather.12
where the time goes:
time: 490 us; the launch traced here: 481 us
  waiting for transfers between devices  322 us (66%)
  matrix products  73 us (15%)
  local copies, waits for them, and re-layouts  30.3 us (6%)
  other arithmetic  24.6 us (5%)
  blocking collectives  16.2 us (3%)
  between operations  14 us (3%)
    psum x1, waiting for transfers between devices, body(): lax.psum(partial_sum.astype(jnp.bfloat16), 'blk').astype(jnp.float32)  73.7 us
    all_gather x1, waiting for transfers between devices, body(): lax.all_gather(w_qkv, 'tok', axis=1, tiled=True)  53.1 us
    all_gather x1, waiting for transfers between devices, body(): lax.all_gather(normed_two, 'blk', axis=0, tiled=True)  41.5 us
    all_gather x1, waiting for transfers between devices, body(): out_full = lax.all_gather(w_out, 'tok', axis=1, tiled=True)  40.5 us
    all_gather x1, waiting for transfers between devices, body(): normed_all = lax.all_gather(normed_one, 'blk', axis=0, tiled=True)  39.4 us
    reduce_scatter x1, waiting for transfers between devices, body(): lax.psum_scatter(jnp.dot(attended, out_full, preferred_element_type=jnp.f...  38.9 us
    all_gather x1, waiting for transfers between devices, body(): lax.all_gather(w_proj, 'tok', axis=0, tiled=True)  33.5 us
    dot_general x1, matrix products, body(): partial_sum = jnp.dot(hidden_act, w_fc2, preferred_element_type=jnp.float32)  28.8 us
  transfers between devices with their start and end apart: 7, of which 7 were waited for; matrix products, arithmetic and copies ran while one was open for 8% of the time, Pallas kernels for 0%

commit v1 on v0

--- a/solution.py
+++ b/solution.py
@@ -43,7 +43,16 @@
     head_cols = w_qkv.shape[2]
     heads_here = head_cols // HD
     normed_one = layer_norm(tok_block, ln1_gain, ln1_bias).astype(jnp.bfloat16)
-    normed_all = lax.all_gather(normed_one, "blk", axis=0, tiled=True)
+    ways = lax.axis_size("blk")
+    up = [(d, (d + 1) % ways) for d in range(ways)]
+    down = [(d, (d - 1) % ways) for d in range(ways)]
+    earlier, later = ([normed_one], [normed_one])
+    for _ in range(ways // 2):
+        earlier.append(lax.ppermute(earlier[-1], "blk", up))
+    for _ in range((ways - 1) // 2):
+        later.append(lax.ppermute(later[-1], "blk", down))
+    line = jnp.concatenate([*earlier[::-1], *later[1:]], axis=0)
+    normed_all = jnp.roll(line, (lax.axis_index("blk") - ways // 2) * normed_one.shape[0], axis=0)
     all_rows = normed_all.shape[0]
     columns = normed_all
     projected_qkv = jnp.einsum(

time: 490 us -> 439 us (0.90); the launches traced: 481 us -> 436 us
  waiting for transfers between devices: 322 us -> 264 us
  local copies, waits for them, and re-layouts: 30.3 us -> 35.3 us
    all_gather x1, waiting for transfers between devices: 40.5 us -> 0.01 us  [body(): out_full = lax.all_gather(w_out, 'tok', axis=1, tiled=True)]
    all_gather x1 -> x0, waiting for transfers between devices: 39.4 us -> none  [body(): normed_all = lax.all_gather(normed_one, 'blk', axis=0, tiled=True)]
    ppermute x0 -> x3, waiting for transfers between devices: none -> 35 us  [the longest x2 35 us: body(): earlier.append(lax.ppermute(earlier[-1], 'blk', up))]
    all_gather x1, waiting for transfers between devices: 53.1 us -> 39.9 us  [body(): lax.all_gather(w_qkv, 'tok', axis=1, tiled=True)]
    unnamed x37 -> x48, local copies, waits for them, and re-layouts: 8.1 us -> 14.2 us
  transfers between devices with their start and end apart: 7 -> 9, of which waited for: 7 -> 7; matrix products, arithmetic and copies ran while one was open for 8% -> 11% of each run, Pallas kernels for 0% -> 0%
where the time goes in v1:
time: 439 us; the launch traced here: 436 us
  waiting for transfers between devices  264 us (60%)
  matrix products  74.3 us (17%)
  local copies, waits for them, and re-layouts  35.3 us (8%)
  other arithmetic  27.2 us (6%)
  blocking collectives  16.2 us (4%)
  between operations  14.1 us (3%)
  starting transfers between devices  5.08 us (1%)
    psum x1, waiting for transfers between devices, body(): lax.psum(partial_sum.astype(jnp.bfloat16), 'blk').astype(jnp.float32)  73.9 us
    all_gather x1, waiting for transfers between devices, body(): lax.all_gather(normed_two, 'blk', axis=0, tiled=True)  41.5 us
    all_gather x1, waiting for transfers between devices, body(): lax.all_gather(w_qkv, 'tok', axis=1, tiled=True)  39.9 us
    reduce_scatter x1, waiting for transfers between devices, body(): lax.psum_scatter(jnp.dot(attended, out_full, preferred_element_type=jnp.f...  38.9 us
    ppermute x2, waiting for transfers between devices, body(): earlier.append(lax.ppermute(earlier[-1], 'blk', up))  35 us
    all_gather x1, waiting for transfers between devices, body(): lax.all_gather(w_proj, 'tok', axis=0, tiled=True)  33.4 us
    dot_general x1, matrix products, body(): partial_sum = jnp.dot(hidden_act, w_fc2, preferred_element_type=jnp.float32)  28.6 us
    all_to_all x1, blocking collectives, body(): lax.all_to_all(outgoing, 'tok', split_axis=0, concat_axis=0, tiled=True)  16.2 us
  transfers between devices with their start and end apart: 9, of which 7 were waited for; matrix products, arithmetic and copies ran while one was open for 11% of the time, Pallas kernels for 0%

profile of v1, /device:TPU:1, one launch (start us, length us, event | category | flops | bytes accessed | tf_op | source)
XLA Modules:
  0.0 436.2 jit_solution(10292976960894705226)
XLA Ops:
  6.5 0.7 all-gather.12.cloned.1.call-update
  7.3 1.7 copy.32
  9.1 1.3 convert_reduce_fusion.1
  10.5 1.5 fusion.44
  12.0 2.5 fusion.47
  14.5 2.0 collective-permute-start
  16.5 19.7 %collective-permute-done = bf16[256,1664]{1,0:T(8,128)(2,1)S(1)} collective-permute-done((bf16[256,1664]{1,0:T(8,128)(2,1)}, bf16[256,1664]{1,0:T(8,128)(2,1)S(1)}, u32[]{:S(2)}, u32[]{:S(2)}) %collective-permute-start) | collective-permute-done | bytes 852000 | tf_op jit(solution)/shard_map/ppermute | solution.py:51
  36.2 0.4 collective-permute-start.1
  36.6 2.5 collective-permute-start.2
  39.0 0.5 broadcast.198
  39.6 1.3 reduce.6
  40.9 15.3 %collective-permute-done.1 = bf16[256,1664]{1,0:T(8,128)(2,1)S(1)} collective-permute-done((bf16[256,1664]{1,0:T(8,128)(2,1)S(1)}, bf16[256,1664]{1,0:T(8,128)(2,1)S(1)}, u32[]{:S(2)}, u32[]{:S(2)}) %collective-permute-start.1) | collective-permute-done | bytes 852000 | tf_op jit(solution)/shard_map/ppermute | solution.py:51
  56.2 1.0 constant_dynamic-update-slice_fusion.7
  57.2 1.0 constant_dynamic-update-slice_fusion.6
  58.2 1.4 constant_dynamic-update-slice_fusion.5
  59.5 1.0 constant_dynamic-update-slice_fusion.4
  60.5 1.0 constant_dynamic-update-slice_fusion.3
  61.5 1.0 constant_dynamic-update-slice_fusion.2
  62.5 1.3 constant_dynamic-update-slice_fusion.1
  63.8 1.0 constant_dynamic-update-slice_fusion
  64.8 3.9 reshape.179
  68.7 39.9 %all-gather.6.cloned.1.call-done = bf16[3,1664,416]{2,0,1:T(4,128)(2,1)} async-done(((bf16[3,52,416]{2,0,1:T(4,128)(2,1)}), bf16[3,1664,416]{2,0,1:T(4,128)(2,1)}) %all-gather.6.cloned.1.call-update) | async-done | bytes 4153360 | tf_op jit(solution)/shard_map/all_gather | solution.py:61
  108.6 9.2 %fusion.35 = bf16[3,1024,416]{1,2,0:T(8,128)(2,1)S(1)} fusion(f32[3,416]{1,0:T(4,128)S(1)} %copy-done.15, bf16[3,1664,416]{2,0,1:T(4,128)(2,1)} %all-gather.6.cloned.1.call-done, bf16[2048,1664]{1,0:T(8,128)(2,1)} %constant_dynamic-update-slice_fusion, s32[]{:T(128)S(6)} %select_n.59), kind=kOutput, calls=%fused_computation.54 | convolution fusion | flops 4255580160 | bytes 12784516 | tf_op jit(solution)/shard_map/td,cde->cte/dot_general | solution.py:58
  117.8 1.1 fusion.98
  118.9 0.6 reshape_squeeze.10
  119.5 1.0 copy.34
  120.5 15.2 %while.10 = (s32[]{:T(128)}, bf16[2,512,4,104]{1,3,2,0:T(8,128)(2,1)}, s32[2,512]{1,0:T(2,128)S(1)}, s32[1,1024]{1,0:T(1,128)S(1)}, bf16[2,512,4,104]{1,3,2,0:T(...) while((s32[]{:T(128)}, bf16[2,512,4,104]{1,3,2,0:T(8,128)(2,1)}, ...), condition=%wide.region_8.9_spmd, body=%wide.region_6.8_spmd.sunk | while | flops 887830528 | bytes 20933720 | solution.py:87
  120.6 0.4 broadcast_compare_fusion.2
  120.9 4.0 fusion.114
  124.9 3.2 fusion.115
  128.1 0.4 broadcast_compare_fusion.2
  128.5 3.8 fusion.114
  132.3 3.2 fusion.115
  135.7 2.0 copy.35
  137.8 0.2 copy.40
  138.0 3.9 convolution_convert_fusion
  142.0 38.9 %reduce-scatter.2.cloned.1.call-done = bf16[256,1664]{1,0:T(8,128)(2,1)} async-done(((bf16[1024,1664]{1,0:T(8,128)(2,1)}), bf16[256,1664]{1,0:T(8,128)(2,1)}) %reduce-scatter.2.cloned.1.call-update) | async-done | bytes 851984 | tf_op jit(solution)/shard_map/reduce_scatter | solution.py:89
  180.9 1.5 fusion.58
  182.4 1.7 multiply_reduce_fusion
  184.1 2.6 add_convert_fusion.2
  186.8 41.5 %all-gather.8.cloned.1.call-done = bf16[1024,1664]{1,0:T(8,128)(2,1)} async-done(((bf16[256,1664]{1,0:T(8,128)(2,1)}), bf16[1024,1664]{1,0:T(8,128)(2,1)}) %all-gather.8.cloned.1.call-update) | async-done | bytes 3407888 | tf_op jit(solution)/shard_map/all_gather | solution.py:99
  228.3 11.3 %fusion.99 = f32[1024,2048]{1,0:T(8,128)S(1)} fusion(bf16[1024,1664]{1,0:T(8,128)(2,1)} %all-gather.8.cloned.1.call-done, bf16[1664,2048]{1,0:T(8,128)(2,1)} %param.34), kind=kOutput, calls=%fused_computation.143 | convolution fusion | flops 6979321856 | bytes 18612224 | tf_op jit(solution)/shard_map/dot_general | solution.py:98
  239.6 28.6 %fusion.29 = f32[1024,1664]{1,0:T(8,128)S(1)} fusion(bf16[2048,1664]{1,0:T(8,128)(2,1)} %param.36, f32[1024,2048]{1,0:T(8,128)S(1)} %fusion.99, f32[2048]{0:T(1024)S(1)} %copy-done.16), kind=kOutput, calls=%fused_computation.48 | convolution fusion | flops 7117733888 | bytes 22028288 | tf_op jit(solution)/shard_map/dot_general | solution.py:106
  268.3 0.4 add_dynamic-update-slice_fusion
  268.8 2.2 convert_element_type.78
  271.0 0.5 all-gather.10.cloned.1.call-update
  271.6 0.1 copy.36
  271.9 1.4 gather_fusion
  273.4 0.6 reduce-window.6
  274.0 0.2 slice_reduce_fusion
  274.2 0.2 copy.31
  274.4 0.9 broadcast_in_dim.40
  275.4 2.0 copy.39
  277.5 73.9 %all-reduce.2.cloned.1.call-done = bf16[1024,1664]{1,0:T(8,128)(2,1)} async-done(((bf16[1024,1664]{1,0:T(8,128)(2,1)}), bf16[1024,1664]{1,0:T(8,128)(2,1)}) %all-reduce.2.cloned.1.call-update) | async-done | bytes 3407888 | tf_op jit(solution)/shard_map/psum | solution.py:110
  351.3 2.8 convert_reduce_fusion
  354.2 3.2 fusion.23
  357.4 1.8 fusion.26
  359.3 5.9 %gather_fusion.1 = bf16[1024,1664]{1,0:T(8,128)(2,1)} fusion(bf16[1024,1664]{1,0:T(8,128)(2,1)S(1)} %fusion.26, s32[1024]{0:T(1024)S(1)} %broadcast_clamp_fusion), kind=kCustom, calls=%fused_computation.1 | custom fusion | bytes 6819840 | tf_op jit(solution)/shard_map/jit(_take)/gather | solution.py:115
  365.1 5.4 %gather.15 = bf16[256,6656]{1,0:T(8,128)(2,1)S(1)} reshape(bf16[1024,1664]{1,0:T(8,128)(2,1)} %gather_fusion.1) | data formatting | bytes 6815744 | tf_op jit(solution)/shard_map/jit(_take)/gather | solution.py:115
  370.6 33.4 %all-gather.10.cloned.1.call-done = bf16[6656,416]{1,0:T(8,128)(2,1)} async-done(((bf16[208,416]{1,0:T(8,128)(2,1)}), bf16[6656,416]{1,0:T(8,128)(2,1)}) %all-gather.10.cloned.1.call-update) | async-done | bytes 5537808 | tf_op jit(solution)/shard_map/all_gather | solution.py:121
  403.9 7.0 %convolution_convert_fusion.1 = bf16[512,416]{0,1:T(8,128)(2,1)} fusion(bf16[6656,416]{1,0:T(8,128)(2,1)} %all-gather.10.cloned.1.call-done, pred[256,6656]{1,0:T(8,128)(4,1)} %bitcast.122, bf16[256,6656]{1,0:T(8,128)(2,1)S(1)} %gather.15, s32[256]{0:T(256)S(1)} %multiply_add_fusion, f32[416]{0:T(512)S(1)} %copy-done.17), kind=kOutput, calls=%fused_computation.70 | convolution fusion | flops 1528987648 | bytes 11078272 | tf_op jit(solution)/shard_map/dot_general | solution.py:142
  410.9 1.2 copy.37
  412.1 16.2 %all_to_all.5 = bf16[32,16,416]{2,1,0:T(8,128)(2,1)S(1)} all-to-all(bf16[32,16,416]{2,1,0:T(8,128)(2,1)S(1)} %bitcast.120), channel_id=1, replica_groups=mesh['blk'=4,'tok'=32] {'tok'}, dimensions={0} | all-to-all | bytes 851968 | tf_op jit(solution)/shard_map/all_to_all | solution.py:144
  428.3 0.8 copy.63
  (71 shorter events, 0.8 us)
Async XLA Ops:
  6.5 51.6 %copy-start.1 = (bf16[1,256,1664]{2,1,0:T(8,128)(2,1)S(1)}, bf16[1,256,1664]{2,1,0:T(8,128)(2,1)}, u32[]{:S(2)}) copy-start(bf16[1,256,1664]{2,1,0:T(8,128)(2,1)} %param.22) | copy-start | bytes 2555908
  6.5 51.6 %copy-start.7 = (f32[1664]{0:T(1024)S(1)}, f32[1664]{0:T(1024)}, u32[]{:S(2)}) copy-start(f32[1664]{0:T(1024)} %param.26) | copy-start | bytes 19972
  6.5 51.6 %copy-start.6 = (f32[1664]{0:T(1024)S(1)}, f32[1664]{0:T(1024)}, u32[]{:S(2)}) copy-start(f32[1664]{0:T(1024)} %param.27) | copy-start | bytes 19972
  6.5 58.3 %all-gather.12.cloned.1.call-start = ((), (), s32[]{:S(2)}) async-start(), calls=%async_computation.7 | async-start | bytes 1892352 | tf_op jit(solution)/shard_map/all_gather | solution.py:88
  7.3 101.3 %all-gather.6.cloned.1.call-start = ((), (), s32[]{:S(2)}) async-start(), calls=%async_computation.2 | async-start | bytes 7028736 | tf_op jit(solution)/shard_map/all_gather | solution.py:61
  9.0 171.8 %reduce-scatter.2.cloned.1.call-start = ((), (), s32[]{:S(2)}) async-start(), calls=%async_computation.3 | async-start | bytes 4259840 | tf_op jit(solution)/shard_map/reduce_scatter | solution.py:89
  14.5 21.7 %collective-permute-start = (bf16[256,1664]{1,0:T(8,128)(2,1)}, bf16[256,1664]{1,0:T(8,128)(2,1)S(1)}, u32[]{:S(2)}, u32[]{:S(2)}) collective-permute-start(bf16[256,1664]{1,0:T(8,128)(2,1)} %fusion.47), channel_id=1, source_target_pairs={{0,32},{32,64},{64,96},{96,0},{1,33},{33,65},{65,97},{97,1},{2,34}... | collective-permute-start | bytes 2555912 | tf_op jit(solution)/shard_map/ppermute | solution.py:51
  36.2 20.0 %collective-permute-start.1 = (bf16[256,1664]{1,0:T(8,128)(2,1)S(1)}, bf16[256,1664]{1,0:T(8,128)(2,1)S(1)}, u32[]{:S(2)}, u32[]{:S(2)}) collective-permute-start(bf16[256,1664]{1,0:T(8,128)(2,1)S(1)} %collective-permute-done), channel_id=1, source_target_pairs={{0,32},{32,64},{64,96},{96,0},{1,33},{33,65},{65,97},{97,1},{2,34}... | collective-permute-start | bytes 2555912 | tf_op jit(solution)/shard_map/ppermute | solution.py:51
  36.6 23.0 %collective-permute-start.2 = (bf16[256,1664]{1,0:T(8,128)(2,1)}, bf16[256,1664]{1,0:T(8,128)(2,1)S(1)}, u32[]{:S(2)}, u32[]{:S(2)}) collective-permute-start(bf16[256,1664]{1,0:T(8,128)(2,1)} %fusion.47), channel_id=1, source_target_pairs={{0,96},{32,0},{64,32},{96,64},{1,97},{33,1},{65,33},{97,65},{2,98}... | collective-permute-start | bytes 2555912 | tf_op jit(solution)/shard_map/ppermute | solution.py:53
  58.2 50.4 %copy-start.15 = (f32[3,416]{1,0:T(4,128)S(1)}, f32[3,416]{1,0:T(4,128)}, u32[]{:S(2)}) copy-start(f32[3,416]{1,0:T(4,128)} %param.29) | copy-start | bytes 14980
  117.8 2.8 copy-start
  120.5 17.4 %copy-start.4 = (bf16[1664,416]{1,0:T(8,128)(2,1)S(1)}, bf16[1664,416]{1,0:T(8,128)(2,1)}, u32[]{:S(2)}) copy-start(bf16[1664,416]{1,0:T(8,128)(2,1)} %reshape.179) | copy-start | bytes 4153348
  138.0 42.9 %copy-start.5 = (f32[1664]{0:T(1024)S(1)}, f32[1664]{0:T(1024)}, u32[]{:S(2)}) copy-start(f32[1664]{0:T(1024)} %param.31) | copy-start | bytes 19972
  141.9 42.2 %copy-start.10 = (f32[1664]{0:T(1024)S(1)}, f32[1664]{0:T(1024)}, u32[]{:S(2)}) copy-start(f32[1664]{0:T(1024)} %param.33) | copy-start | bytes 19972
  141.9 42.2 %copy-start.11 = (f32[1664]{0:T(1024)S(1)}, f32[1664]{0:T(1024)}, u32[]{:S(2)}) copy-start(f32[1664]{0:T(1024)} %param.32) | copy-start | bytes 19972
  141.9 86.3 %all-gather.8.cloned.1.call-start = ((), (), s32[]{:S(2)}) async-start(), calls=%async_computation.4 | async-start | bytes 4259840 | tf_op jit(solution)/shard_map/all_gather | solution.py:99
  186.7 164.6 %all-reduce.2.cloned.1.call-start = ((), (), s32[]{:S(2)}) async-start(), calls=%async_computation.5 | async-start | bytes 6815744 | tf_op jit(solution)/shard_map/psum | solution.py:110
  186.8 52.8 %copy-start.16 = (f32[2048]{0:T(1024)S(1)}, f32[2048]{0:T(1024)}, u32[]{:S(2)}) copy-start(f32[2048]{0:T(1024)} %param.35) | copy-start | bytes 24580
  239.6 28.7 %copy-start.3 = (bf16[256,1664]{1,0:T(8,128)(2,1)S(1)}, bf16[256,1664]{1,0:T(8,128)(2,1)}, u32[]{:S(2)}) copy-start(bf16[256,1664]{1,0:T(8,128)(2,1)} %reduce-scatter.2.cloned.1.call-done) | copy-start | bytes 2555908
  268.7 2.8 copy-start.9
  268.8 4.5 %copy-start.14 = (s32[1,32]{1,0:T(1,128)S(1)}, s32[1,32]{1,0:T(1,128)}, u32[]{:S(2)}) copy-start(s32[1,32]{1,0:T(1,128)} %param.25) | copy-start | bytes 388
  270.9 80.4 %copy-start.8 = (f32[1664]{0:T(1024)S(1)}, f32[1664]{0:T(1024)}, u32[]{:S(2)}) copy-start(f32[1664]{0:T(1024)} %param.37) | copy-start | bytes 19972
  271.0 133.0 %all-gather.10.cloned.1.call-start = ((), (), s32[]{:S(2)}) async-start(), calls=%async_computation.6 | async-start | bytes 7028736 | tf_op jit(solution)/shard_map/all_gather | solution.py:121
  271.6 85.8 %copy-start.12 = (f32[1664]{0:T(1024)S(1)}, f32[1664]{0:T(1024)}, u32[]{:S(2)}) copy-start(f32[1664]{0:T(1024)} %param.39) | copy-start | bytes 19972
  271.6 85.8 %copy-start.13 = (f32[1664]{0:T(1024)S(1)}, f32[1664]{0:T(1024)}, u32[]{:S(2)}) copy-start(f32[1664]{0:T(1024)} %param.38) | copy-start | bytes 19972
  351.3 6.1 %copy-start.2 = (bf16[1024,1664]{1,0:T(8,128)(2,1)S(1)}, bf16[1024,1664]{1,0:T(8,128)(2,1)}, u32[]{:S(2)}) copy-start(bf16[1024,1664]{1,0:T(8,128)(2,1)} %all-reduce.2.cloned.1.call-done) | copy-start | bytes 10223620
  365.1 38.8 %copy-start.17 = (f32[416]{0:T(512)S(1)}, f32[416]{0:T(512)}, u32[]{:S(2)}) copy-start(f32[416]{0:T(512)} %param.41) | copy-start | bytes 4996
Sparse Core Ops, SparseCore 0:
  9.6 47.2 all-gather.11
  59.1 49.3 all-gather.5
  142.1 38.7 reduce-scatter.1
  186.8 41.3 all-gather.7
  271.1 80.1 all-reduce.1
  353.4 50.4 all-gather.9
